TPU v7x, 128 devices: a whole 4x4x4 slice. The times are simulated.
128 devices in a mesh: ka: 64 (over y, z, x_lo, core), pa: 2 (over x_hi).
Axes of the slice: x: 4 (x_hi: 2, x_lo: 2; x = x_hi * 2 + x_lo), y: 4, z: 4, core: 2. Of those that a mesh axis runs over, the one named last changes fastest.
Arguments:
- conduction: bfloat16 [64, 48, 2048], P('ka'), may hold values from -6 to 6
- weighted: bfloat16 [64, 48, 2048], P('ka'), may hold values from -6 to 6
- valence: bfloat16 [64, 64, 2048], P('ka', None, 'pa'), may hold values from -0.015625 to 0.015625
- screening: bfloat16 [64, 2048, 2048], P('ka', None, 'pa'), may hold values from -0.125 to 0.125
- pair_transfer: int32 [64, 64], replicated, may hold values from 0 to 63, as said below
- owner_map: int32 [64], replicated, may hold values from 0 to 63, each once
Outputs:
- kernel_out: float32 [64, 48, 64], P('ka')
Inputs may be any that keep to these rules, and one draw needn't show every extreme that they name: pair_transfer[i, j] = (g_i - g_j) mod 64 for positions g of the k-points on a cyclic grid of 64 points (a permutation drawn from the seed), so each row and each column names every transfer once. `owner_map`: each transfer is held by exactly one slot.
All inputs are finite; a program needn't handle non-finite values.
Results may differ from a plain program's by a relative error of at most 0.0029.
Values may be sent and summed in bfloat16 or wider, within the bound.
No kernel may reach another device: no remote copies, remote signals or barrier semaphores. Data moves between devices by JAX's collectives and lax.ppermute only.
A program may use at most 128 MiB of HBM per device.

v0:
```python
import jax
import jax.numpy as jnp
from jax import lax
from jax.sharding import PartitionSpec as P


def in_blocks(x, dim, peers):
    before, after = (x.shape[:dim], x.shape[dim + 1 :])
    return jnp.moveaxis(x.reshape(*before, peers, -1, *after), dim, 0)


def sent_and_summed(x, axis, dim):
    peers = lax.axis_size(axis)
    blocks = lax.all_to_all(in_blocks(x, dim, peers), axis, 0, 0, tiled=True)
    return jnp.sum(blocks, axis=0)


def over_pieces(x, axis):
    return lax.all_gather(x, axis).sum(0)


def shards(conduction, weighted, valence, screening, pair_transfer, owner_map):
    local_count = conduction.shape[0]
    half_width = screening.shape[2]
    first_column = lax.axis_index("pa") * half_width
    first_slot = lax.axis_index("ka") * local_count
    owned_transfers = lax.dynamic_slice_in_dim(owner_map, first_slot, local_count)
    columns = jnp.arange(pair_transfer.shape[1], dtype=jnp.int32)
    matches = pair_transfer[None, :, :] == owned_transfers[:, None, None]
    partners = jnp.sum(jnp.where(matches, columns[None, None, :], 0), axis=2)
    every_cond = lax.all_gather(conduction, "ka", axis=0, tiled=True)
    piece = lax.all_gather(weighted, "ka", axis=0, tiled=True)
    count = piece.shape[0]
    total = jnp.zeros((count, piece.shape[1], half_width), jnp.float32)
    partner_rows = partners[0]
    partner_cond = jnp.take(every_cond, partner_rows, axis=0)
    density = (partner_cond.astype(jnp.float32) * piece.astype(jnp.float32)).astype(jnp.bfloat16)
    screened = jnp.dot(
        density.reshape(-1, density.shape[2]), screening[0], preferred_element_type=jnp.float32
    )
    partner_half = lax.dynamic_slice_in_dim(partner_cond, first_column, half_width, 2)
    total = partner_half.astype(jnp.float32) * screened.reshape(total.shape)
    every_valence = lax.all_gather(valence, "ka", axis=0, tiled=True)
    owner_terms = jnp.einsum(
        "kbp,kvp->kbv", total, every_valence.astype(jnp.float32), precision=lax.Precision.HIGHEST
    )
    partial_out = sent_and_summed(owner_terms, "ka", 0)
    return over_pieces(partial_out, "pa")


def solution(mesh):
    in_specs = (
        P("ka", None, None),
        P("ka", None, None),
        P("ka", None, "pa"),
        P("ka", None, "pa"),
        P(),
        P(),
    )
    out_specs = P("ka", None, None)
    return jax.shard_map(shards, mesh=mesh, in_specs=in_specs, out_specs=out_specs, check_vma=False)
```

profile of v0, /device:TPU:0, one launch (start us, length us, event | category | flops | bytes accessed | tf_op | source)
XLA Modules:
  0.0 408.6 jit_solution(18051606673469656491)
XLA Ops:
  6.5 0.0 all-gather.5.cloned.1.call-start
  6.5 0.7 all-gather.5.cloned.1.call-update
  7.3 0.0 all-gather.7.cloned.1.call-start
  7.3 0.7 all-gather.7.cloned.1.call-update
  8.0 0.0 all-gather.9.cloned.1.call-start
  8.1 0.7 all-gather.9.cloned.1.call-update
  8.7 1.2 dynamic_slice.6
  10.0 1.5 select_reduce_fusion
  11.5 116.5 %all-gather.5.cloned.1.call-done = bf16[64,48,2048]{2,1,0:T(8,128)(2,1)} async-done(((bf16[1,48,2048]{2,1,0:T(8,128)(2,1)}), bf16[64,48,2048]{2,1,0:T(8,128)(2,1)}) %all-gather.5.cloned.1.call-update) | async-done | bytes 12582928 | tf_op jit(solution)/shard_map/all_gather | solution.py:31
  128.1 12.1 %gather_fusion = bf16[64,48,2048]{2,1,0:T(8,128)(2,1)} fusion(bf16[64,48,2048]{2,1,0:T(8,128)(2,1)} %all-gather.5.cloned.1.call-done, s32[1024]{0:T(1024)S(1)} %pad_clamp_fusion), kind=kCustom, calls=%fused_computation | custom fusion | bytes 25166080 | tf_op jit(solution)/shard_map/jit(_take)/gather | solution.py:36
  140.1 10.9 %broadcast_select_fusion = bf16[64,48,2048]{2,1,0:T(8,128)(2,1)} fusion(bf16[64,48,2048]{2,1,0:T(8,128)(2,1)} %gather_fusion, pred[64]{0:T(512)(128)(4,1)S(1)} %compare_and_fusion), kind=kLoop, calls=%fused_computation.6 | loop fusion | flops 6291456 | bytes 25165888 | tf_op jit(solution)/shard_map/jit(_take)/select_n | solution.py:36
  151.0 94.0 %all-gather.7.cloned.1.call-done = bf16[64,48,2048]{2,1,0:T(8,128)(2,1)} async-done(((bf16[1,48,2048]{2,1,0:T(8,128)(2,1)}), bf16[64,48,2048]{2,1,0:T(8,128)(2,1)}) %all-gather.7.cloned.1.call-update) | async-done | bytes 12582928 | tf_op jit(solution)/shard_map/all_gather | solution.py:32
  245.0 21.8 %fusion = f32[64,48,1024]{2,1,0:T(8,128)} fusion(bf16[64,48,2048]{2,1,0:T(8,128)(2,1)} %all-gather.7.cloned.1.call-done, bf16[64,48,2048]{2,1,0:T(8,128)(2,1)} %broadcast_select_fusion, bf16[1,2048,1024]{2,1,0:T(8,128)(2,1)} %param.9), kind=kOutput, calls=%fused_computation.2 | convolution fusion | flops 12910067712 | bytes 41943040 | tf_op jit(solution)/shard_map/dot_general | solution.py:38
  266.9 89.3 %all-gather.9.cloned.1.call-done = bf16[64,64,1024]{2,1,0:T(8,128)(2,1)} async-done(((bf16[1,64,1024]{2,1,0:T(8,128)(2,1)}), bf16[64,64,1024]{2,1,0:T(8,128)(2,1)}) %all-gather.9.cloned.1.call-update) | async-done | bytes 8388624 | tf_op jit(solution)/shard_map/all_gather | solution.py:43
  356.2 13.1 %fusion.6 = f32[64,1,48,64]{3,2,1,0:T(8,128)S(1)} fusion(bf16[64,64,1024]{2,1,0:T(8,128)(2,1)} %all-gather.9.cloned.1.call-done, f32[64,48,1024]{2,1,0:T(8,128)} %fusion, bf16[64,48,2048]{2,1,0:T(8,128)(2,1)} %broadcast_select_fusion, s32[]{:T(128)S(6)} %select_n.36), kind=kOutput, calls=%fused_computation.9 | convolution fusion | flops 2422210560 | bytes 28049412 | tf_op jit(solution)/shard_map/kbp,kvp->kbv/dot_general | solution.py:44
  369.3 1.0 reshape.50
  370.3 21.6 %all_to_all.5 = f32[64,1,3072]{2,1,0:T(1,128)S(1)} all-to-all(f32[64,1,3072]{2,1,0:T(1,128)S(1)} %reshape.50), channel_id=1, replica_groups=mesh['ka'=64,'pa'=2] {'ka'}, dimensions={0} | all-to-all | bytes 1572864 | tf_op jit(solution)/shard_map/all_to_all | solution.py:14
  391.9 0.5 broadcast.33
  392.4 2.5 reduce.5
  394.9 0.4 reshape.51
  395.3 0.1 reduce_sum.33
  395.5 6.0 %all-gather = f32[96,64]{1,0:T(8,128)S(1)} all-gather(f32[48,64]{1,0:T(8,128)S(1)} %reduce_sum.33), channel_id=2, replica_groups=mesh['ka'=64,'pa'=2] {'pa'}, dimensions={0}, use_global_device_ids=true | all-gather | bytes 36864 | tf_op jit(solution)/shard_map/all_gather | solution.py:19
  401.5 0.6 reduce.4
  (3 shorter events, 0.0 us)
Async XLA Ops:
  6.5 121.5 %all-gather.5.cloned.1.call-start = ((), (), s32[]{:S(2)}) async-start(), calls=%async_computation.1 | async-start | bytes 12779520 | tf_op jit(solution)/shard_map/all_gather | solution.py:31
  7.3 237.8 %all-gather.7.cloned.1.call-start = ((), (), s32[]{:S(2)}) async-start(), calls=%async_computation.2 | async-start | bytes 12779520 | tf_op jit(solution)/shard_map/all_gather | solution.py:32
  8.0 348.2 %all-gather.9.cloned.1.call-start = ((), (), s32[]{:S(2)}) async-start(), calls=%async_computation.3 | async-start | bytes 8519680 | tf_op jit(solution)/shard_map/all_gather | solution.py:43
Sparse Core Ops, SparseCore 0:
  9.0 118.9 all-gather.4
  129.8 115.2 all-gather.6
  246.8 109.4 all-gather.8
where the time goes:
time: 409 us
  waiting for transfers between devices  302 us (74%)
  matrix products  34.9 us (9%)
  blocking collectives  27.6 us (7%)
  other arithmetic  15.7 us (4%)
  local copies, waits for them, and re-layouts  15.2 us (4%)
  between operations  13.2 us (3%)
    all_gather x1, waiting for transfers between devices, shards(): every_cond = lax.all_gather(conduction, 'ka', axis=0, tiled=True)  117 us
    all_gather x1, waiting for transfers between devices, shards(): piece = lax.all_gather(weighted, 'ka', axis=0, tiled=True)  94 us
    all_gather x1, waiting for transfers between devices, shards(): every_valence = lax.all_gather(valence, 'ka', axis=0, tiled=True)  89.3 us
    dot_general x1, matrix products, shards(): jnp.dot(density.reshape(-1, density.shape[2]), screening[0], preferred_el...  21.8 us
    all_to_all x1, blocking collectives, sent_and_summed(): blocks = lax.all_to_all(in_blocks(x, dim, peers), axis, 0, 0, tiled=True)  21.6 us
    dot_general x1, matrix products, shards(): jnp.einsum('kbp,kvp->kbv', total, every_valence.astype(jnp.float32), prec...  13.1 us
    gather x1, local copies, waits for them, and re-layouts, shards(): partner_cond = jnp.take(every_cond, partner_rows, axis=0)  12.1 us
    select_n x2, other arithmetic, shards(): partner_cond = jnp.take(every_cond, partner_rows, axis=0)  10.9 us
  transfers between devices with their start and end apart: 3, of which 3 were waited for; matrix products, arithmetic and copies ran while one was open for 12% of the time, Pallas kernels for 0%

commit v1 on v0

--- a/solution.py
+++ b/solution.py
@@ -2,6 +2,11 @@
 import jax.numpy as jnp
 from jax import lax
 from jax.sharding import PartitionSpec as P
+
+
+def swapped_in(x, axis, along):
+    repeated = jnp.stack([x] * lax.axis_size(axis))
+    return jnp.concatenate(lax.all_to_all(repeated, axis, 0, 0), axis=along)
 
 
 def in_blocks(x, dim, peers):
@@ -29,7 +34,7 @@
     matches = pair_transfer[None, :, :] == owned_transfers[:, None, None]
     partners = jnp.sum(jnp.where(matches, columns[None, None, :], 0), axis=2)
     every_cond = lax.all_gather(conduction, "ka", axis=0, tiled=True)
-    piece = lax.all_gather(weighted, "ka", axis=0, tiled=True)
+    piece = swapped_in(weighted, "ka", 0)
     count = piece.shape[0]
     total = jnp.zeros((count, piece.shape[1], half_width), jnp.float32)
     partner_rows = partners[0]

time: 409 us -> 441 us (1.078)
  waiting for transfers between devices: 302 us -> 328 us
  other arithmetic: 15.7 us -> 4.03 us
  starting transfers between devices: 0.08 us -> 10.4 us
  local copies, waits for them, and re-layouts: 15.2 us -> 21.4 us
    all_gather x1, waiting for transfers between devices: 117 us -> 248 us  [shards(): every_cond = lax.all_gather(conduction, 'ka', axis=0, tiled=True)]
    all_gather x1 -> x0, waiting for transfers between devices: 94 us -> none  [shards(): piece = lax.all_gather(weighted, 'ka', axis=0, tiled=True)]
    select_n x2 -> x1, other arithmetic: 10.9 us -> 0.01 us  [shards(): partner_cond = jnp.take(every_cond, partner_rows, axis=0)]
    all_gather x1, waiting for transfers between devices: 89.3 us -> 78.6 us  [shards(): every_valence = lax.all_gather(valence, 'ka', axis=0, tiled=True)]
    all_to_all x0 -> x1, starting transfers between devices: none -> 10.4 us  [swapped_in(): return jnp.concatenate(lax.all_to_all(repeated, axis, 0, 0), axis=along)]
    another operation x0 -> x1, local copies, waits for them, and re-layouts: none -> 6.97 us  [swapped_in(): repeated = jnp.stack([x] * lax.axis_size(axis))]
  transfers between devices with their start and end apart: 3 -> 3, of which waited for: 3 -> 2; matrix products, arithmetic and copies ran while one was open for 12% -> 10% of each run, Pallas kernels for 0% -> 0%
where the time goes in v1:
time: 441 us; the launch traced here: 440 us
  waiting for transfers between devices  328 us (74%)
  matrix products  35.7 us (8%)
  blocking collectives  27.3 us (6%)
  local copies, waits for them, and re-layouts  21.4 us (5%)
  between operations  13.5 us (3%)
  starting transfers between devices  10.4 us (2%)
    all_gather x1, waiting for transfers between devices, shards(): every_cond = lax.all_gather(conduction, 'ka', axis=0, tiled=True)  248 us
    all_gather x1, waiting for transfers between devices, shards(): every_valence = lax.all_gather(valence, 'ka', axis=0, tiled=True)  78.6 us
    dot_general x1, matrix products, shards(): jnp.dot(density.reshape(-1, density.shape[2]), screening[0], preferred_el...  22.1 us
    all_to_all x1, blocking collectives, sent_and_summed(): blocks = lax.all_to_all(in_blocks(x, dim, peers), axis, 0, 0, tiled=True)  21.3 us
    dot_general x1, matrix products, shards(): jnp.einsum('kbp,kvp->kbv', total, every_valence.astype(jnp.float32), prec...  13.6 us
    gather x1, local copies, waits for them, and re-layouts, shards(): partner_cond = jnp.take(every_cond, partner_rows, axis=0)  11.9 us
    all_to_all x1, starting transfers between devices, swapped_in(): return jnp.concatenate(lax.all_to_all(repeated, axis, 0, 0), axis=along)  10.4 us
  transfers between devices with their start and end apart: 3, of which 2 were waited for; matrix products, arithmetic and copies ran while one was open for 10% of the time, Pallas kernels for 0%

profile of v1, /device:TPU:0, one launch (start us, length us, event | category | flops | bytes accessed | tf_op | source)
XLA Modules:
  0.0 440.3 jit_solution(4870692163867513016)
XLA Ops:
  6.5 0.0 all-gather.4.cloned.1.call-start
  6.5 0.7 all-gather.4.cloned.1.call-update
  7.3 7.0 %stack.2 = bf16[64,1,48,2048]{3,2,1,0:T(8,128)(2,1)} broadcast(bf16[48,2048]{1,0:T(8,128)(2,1)} %bitcast.31), dimensions={2,3} | broadcast | bytes 12779520 | tf_op jit(solution)/shard_map/stack | solution.py:8
  14.2 0.0 copy-start.1
  14.2 0.0 copy-start
  14.2 10.4 %all-to-all-start = ((bf16[64,1,48,2048]{3,2,1,0:T(8,128)(2,1)}), bf16[64,1,48,2048]{3,2,1,0:T(8,128)(2,1)}, u32[]{:S(2)}, u32[]{:S(2)}) async-start(bf16[64,1,48,2048]{3,2,1,0:T(8,128)(2,1)} %stack.2), calls=%async_computation | async-start | bytes 25165824 | tf_op jit(solution)/shard_map/all_to_all | solution.py:9
  24.6 0.0 all-gather.6.cloned.1.call-start
  24.6 0.7 all-gather.6.cloned.1.call-update
  25.4 0.0 copy-done.1
  25.4 0.6 dynamic_slice.6
  26.0 0.0 copy-done
  26.0 0.7 select_reduce_fusion
  26.7 248.0 %all-gather.4.cloned.1.call-done = bf16[64,48,2048]{2,1,0:T(8,128)(2,1)} async-done(((bf16[1,48,2048]{2,1,0:T(8,128)(2,1)}), bf16[64,48,2048]{2,1,0:T(8,128)(2,1)}) %all-gather.4.cloned.1.call-update) | async-done | bytes 12582928 | tf_op jit(solution)/shard_map/all_gather | solution.py:36
  274.8 11.9 %gather_fusion = bf16[64,48,2048]{2,1,0:T(8,128)(2,1)} fusion(bf16[64,48,2048]{2,1,0:T(8,128)(2,1)} %all-gather.4.cloned.1.call-done, s32[1024]{0:T(1024)S(1)} %pad_clamp_fusion), kind=kCustom, calls=%fused_computation | custom fusion | bytes 25166080 | tf_op jit(solution)/shard_map/jit(_take)/gather | solution.py:41
  286.7 0.0 all-to-all-done
  286.7 22.1 %fusion.1 = f32[64,48,1024]{2,1,0:T(8,128)} fusion(bf16[64,1,48,2048]{3,2,1,0:T(8,128)(2,1)} %all-to-all-done, bf16[64,48,2048]{2,1,0:T(8,128)(2,1)} %gather_fusion, pred[64]{0:T(512)(128)(4,1)S(1)} %compare_and_fusion, bf16[1,2048,1024]{2,1,0:T(8,128)(2,1)} %param.9), kind=kOutput, calls=%fused_computation.3 | convolution fusion | flops 12916359168 | bytes 41943104 | tf_op jit(solution)/shard_map/dot_general | solution.py:43
  308.8 78.6 %all-gather.6.cloned.1.call-done = bf16[64,64,1024]{2,1,0:T(8,128)(2,1)} async-done(((bf16[1,64,1024]{2,1,0:T(8,128)(2,1)}), bf16[64,64,1024]{2,1,0:T(8,128)(2,1)}) %all-gather.6.cloned.1.call-update) | async-done | bytes 8388624 | tf_op jit(solution)/shard_map/all_gather | solution.py:48
  387.4 13.6 %fusion.12 = f32[64,1,48,64]{3,2,1,0:T(8,128)S(1)} fusion(bf16[64,64,1024]{2,1,0:T(8,128)(2,1)} %all-gather.6.cloned.1.call-done, f32[64,48,1024]{2,1,0:T(8,128)} %fusion.1, bf16[64,48,2048]{2,1,0:T(8,128)(2,1)} %gather_fusion, s32[]{:T(128)S(6)} %select_n.49, pred[64]{0:T(512)(128)(4,1)S(1)} %compare_and_fusion), kind=kOutput, calls=%fused_computation.15 | convolution fusion | flops 2425356288 | bytes 28049476 | tf_op jit(solution)/shard_map/kbp,kvp->kbv/dot_general | solution.py:49
  401.0 1.0 reshape.81
  401.9 21.3 %all_to_all.10 = f32[64,1,3072]{2,1,0:T(1,128)S(1)} all-to-all(f32[64,1,3072]{2,1,0:T(1,128)S(1)} %reshape.81), channel_id=1, replica_groups=mesh['ka'=64,'pa'=2] {'ka'}, dimensions={0} | all-to-all | bytes 1572864 | tf_op jit(solution)/shard_map/all_to_all | solution.py:19
  423.2 0.5 broadcast.61
  423.8 2.5 reduce.5
  426.3 0.4 reshape.82
  426.7 0.1 reduce_sum.33
  426.8 6.0 %all-gather = f32[96,64]{1,0:T(8,128)S(1)} all-gather(f32[48,64]{1,0:T(8,128)S(1)} %reduce_sum.33), channel_id=2, replica_groups=mesh['ka'=64,'pa'=2] {'pa'}, dimensions={0}, use_global_device_ids=true | all-gather | bytes 36864 | tf_op jit(solution)/shard_map/all_gather | solution.py:24
  432.8 0.6 reduce.4
  (3 shorter events, 0.0 us)
Async XLA Ops:
  6.5 268.2 %all-gather.4.cloned.1.call-start = ((), (), s32[]{:S(2)}) async-start(), calls=%async_computation.2 | async-start | bytes 12779520 | tf_op jit(solution)/shard_map/all_gather | solution.py:36
  14.2 11.1 %copy-start.1 = (s32[64]{0:T(128)S(1)}, s32[64]{0:T(128)}, u32[]{:S(2)}) copy-start(s32[64]{0:T(128)} %param.11) | copy-start | bytes 772
  14.2 11.7 %copy-start = (s32[64,64]{1,0:T(8,128)S(1)}, s32[64,64]{1,0:T(8,128)}, u32[]{:S(2)}) copy-start(s32[64,64]{1,0:T(8,128)} %param.10) | copy-start | bytes 49156
  14.2 272.5 %all-to-all-start = ((bf16[64,1,48,2048]{3,2,1,0:T(8,128)(2,1)}), bf16[64,1,48,2048]{3,2,1,0:T(8,128)(2,1)}, u32[]{:S(2)}, u32[]{:S(2)}) async-start(bf16[64,1,48,2048]{3,2,1,0:T(8,128)(2,1)} %stack.2), calls=%async_computation | async-start | bytes 25165824 | tf_op jit(solution)/shard_map/all_to_all | solution.py:9
  24.6 362.8 %all-gather.6.cloned.1.call-start = ((), (), s32[]{:S(2)}) async-start(), calls=%async_computation.3 | async-start | bytes 8519680 | tf_op jit(solution)/shard_map/all_gather | solution.py:48
Sparse Core Ops, SparseCore 0:
  9.0 265.6 all-gather.3
  276.5 110.8 all-gather.5
